TPU v7x, 256 devices: a whole 4x4x8 slice. The times are simulated.
256 devices in a mesh: grp: 4 (over y_lo, core), trk: 64 (over z, x, y_hi).
Axes of the slice: x: 4, y: 4 (y_hi: 2, y_lo: 2; y = y_hi * 2 + y_lo), z: 8, core: 2. Of those that a mesh axis runs over, the one named last changes fastest.
Arguments:
- fields: bfloat16 [256, 512, 512], P('grp', 'trk'), may hold values from -81 to 81
- upstream: bfloat16 [256, 512, 512], P('grp', 'trk'), may hold values from -6 to 6
- ln_gain: float32 [512], replicated, may hold values from 0.1 to 1.9
- weights: bfloat16 [4, 512, 512], P(None, 'grp', 'trk'), may hold values from -8 to 8
Outputs:
- grad_fields: bfloat16 [256, 512, 512], P('grp', 'trk')
- grad_weights: float32 [4, 512, 512], P(None, 'grp', 'trk')
- grad_gain: float32 [512], replicated
All inputs are finite; a program needn't handle non-finite values.
Results may differ from a plain program's by a relative error of at most 0.014.
The roundings to bfloat16 on the way count: a program that leaves them out, or rounds other values in their place, can miss the bound.
Values may be sent and summed in bfloat16 or wider, within the bound.
A program may use at most 64 MiB of HBM per device.

v0:
```python
import jax
import jax.numpy as jnp
from jax import lax
from jax.sharding import PartitionSpec as P

HEADS = 8


def normalize(fields, ln_gain):
    values = fields.astype(jnp.float32)
    row_mean = jnp.mean(values, -1, keepdims=True)
    offset = values - row_mean
    row_var = jnp.mean(offset * offset, -1, keepdims=True)
    inv_std = lax.rsqrt(row_var + 1e-05)
    centred = offset * inv_std
    normed = (centred * ln_gain).astype(jnp.bfloat16)
    return (normed, centred, inv_std)


def project(normed, w_in):
    return [
        jnp.einsum("rti,ij->rtj", normed, w_in[index], preferred_element_type=jnp.float32).astype(
            jnp.bfloat16
        )
        for index in range(3)
    ]


def split_heads(block, heads):
    rows, length, width = block.shape
    return (
        block.reshape(rows, length, heads, width // heads)
        .transpose(0, 2, 1, 3)
        .reshape(rows * heads, length, width // heads)
    )


def merge_heads(block, rows):
    items, length, size = block.shape
    return (
        block.reshape(rows, items // rows, length, size)
        .transpose(0, 2, 1, 3)
        .reshape(rows, length, items // rows * size)
    )


def head_back(members):
    query, keyed, valued, grad_out = members
    scaling = query.shape[-1] ** (-0.5)
    scores = jnp.einsum("qd,kd->qk", query, keyed, preferred_element_type=jnp.float32) * scaling
    row_max = jnp.max(scores, -1, keepdims=True)
    shifted = jnp.exp(scores - row_max)
    attn_prob = shifted / jnp.sum(shifted, -1, keepdims=True)
    prob_low = attn_prob.astype(jnp.bfloat16)
    output = jnp.einsum("qk,kd->qd", prob_low, valued, preferred_element_type=jnp.float32).astype(
        jnp.bfloat16
    )
    dprobs = jnp.einsum("qd,kd->qk", grad_out, valued, preferred_element_type=jnp.float32)
    row_dot = jnp.sum(attn_prob * dprobs, -1, keepdims=True)
    score_grad = (attn_prob * (dprobs - row_dot) * scaling).astype(jnp.bfloat16)
    grad_value = jnp.einsum(
        "qk,qd->kd", prob_low, grad_out, preferred_element_type=jnp.float32
    ).astype(jnp.bfloat16)
    grad_query = jnp.einsum(
        "qk,kd->qd", score_grad, keyed, preferred_element_type=jnp.float32
    ).astype(jnp.bfloat16)
    grad_key = jnp.einsum(
        "qk,qd->kd", score_grad, query, preferred_element_type=jnp.float32
    ).astype(jnp.bfloat16)
    return (output, grad_query, grad_key, grad_value)


def attend_back(query_proj, key_proj, value_proj, upstream_rows, w_out):
    rows = query_proj.shape[0]
    grad_attended = jnp.einsum(
        "rtj,ij->rti", upstream_rows, w_out, preferred_element_type=jnp.float32
    ).astype(jnp.bfloat16)
    pieces = lax.map(
        head_back,
        (
            split_heads(query_proj, HEADS),
            split_heads(key_proj, HEADS),
            split_heads(value_proj, HEADS),
            split_heads(grad_attended, HEADS),
        ),
    )
    return [merge_heads(piece, rows) for piece in pieces]


def input_grad(grad_query, grad_key, grad_value, w_in, centred, inv_std, ln_gain):
    stacked = jnp.stack([grad_query, grad_key, grad_value], 2)
    grad_normed = jnp.einsum("rtcj,cij->rti", stacked, w_in, preferred_element_type=jnp.float32)
    width = grad_normed.shape[-1]
    gain_term = jnp.sum((grad_normed * centred).reshape(-1, width), 0)
    scaled = grad_normed * ln_gain
    branch = inv_std * (
        scaled
        - jnp.mean(scaled, -1, keepdims=True)
        - centred * jnp.mean(scaled * centred, -1, keepdims=True)
    )
    return (branch.astype(jnp.bfloat16), gain_term)


def proj_grads(normed, grad_query, grad_key, grad_value):
    return [
        jnp.einsum("rti,rtj->ij", normed, member, preferred_element_type=jnp.float32)
        for member in (grad_query, grad_key, grad_value)
    ]


def shards(fields, upstream, ln_gain, weights):
    w_part = lax.all_gather(weights, "trk", axis=2, tiled=True)
    w_full = lax.all_gather(w_part, "grp", axis=1, tiled=True)
    w_in = w_full[:3]
    w_out = w_full[3]
    rows_dev, trk_dev, width = fields.shape
    cell_count = rows_dev * lax.axis_size("grp") * trk_dev * lax.axis_size("trk")
    normed, centred, inv_std = normalize(fields, ln_gain)
    query_proj, key_proj, value_proj = project(normed, w_in)
    query_rows, key_rows, value_rows, upstream_rows = (
        lax.all_to_all(query_proj, "trk", split_axis=0, concat_axis=1, tiled=True),
        lax.all_to_all(key_proj, "trk", split_axis=0, concat_axis=1, tiled=True),
        lax.all_to_all(value_proj, "trk", split_axis=0, concat_axis=1, tiled=True),
        lax.all_to_all(upstream, "trk", split_axis=0, concat_axis=1, tiled=True),
    )
    attended, grad_query, grad_key, grad_value = attend_back(
        query_rows, key_rows, value_rows, upstream_rows, w_out
    )
    back_query, back_key, back_value = (
        lax.all_to_all(grad_query, "trk", split_axis=1, concat_axis=0, tiled=True),
        lax.all_to_all(grad_key, "trk", split_axis=1, concat_axis=0, tiled=True),
        lax.all_to_all(grad_value, "trk", split_axis=1, concat_axis=0, tiled=True),
    )
    grad_list = proj_grads(normed, back_query, back_key, back_value)
    branch_cells, gain_term = input_grad(
        back_query, back_key, back_value, w_in, centred, inv_std, ln_gain
    )
    out_grad = jnp.einsum(
        "rti,rtj->ij", attended, upstream_rows, preferred_element_type=jnp.float32
    )
    raw_grad = jnp.stack(grad_list + [out_grad])
    partial_grad = lax.psum_scatter(
        raw_grad.astype(jnp.bfloat16), "grp", scatter_dimension=1, tiled=True
    ).astype(jnp.float32)
    summed_grad = lax.psum_scatter(partial_grad, "trk", scatter_dimension=2, tiled=True)
    gain_sum = lax.psum(gain_term, ("grp", "trk"))
    factor = float(cell_count) ** (-0.5)
    grad_fields = (upstream.astype(jnp.float32) + branch_cells.astype(jnp.float32)).astype(
        jnp.bfloat16
    )
    return (grad_fields, summed_grad * factor, gain_sum * factor)


def solution(mesh):
    in_specs = (P("grp", "trk", None), P("grp", "trk", None), P(), P(None, "grp", "trk"))
    out_specs = (P("grp", "trk", None), P(None, "grp", "trk"), P())
    return jax.shard_map(shards, mesh=mesh, in_specs=in_specs, out_specs=out_specs, check_vma=False)
```

profile of v0, /device:TPU:2, one launch (start us, length us, event | category | flops | bytes accessed | tf_op | source)
XLA Modules:
  0.0 1188.6 jit_solution(13073194801549360445)
XLA Ops:
  8.0 184.0 %all_gather.6 = bf16[4,128,512]{1,0,2:T(4,128)(2,1)S(1)} all-gather(bf16[4,128,8]{1,0,2:T(4,128)(2,1)S(1)} %copy.57), channel_id=1, replica_groups=mesh['grp'=4,'trk'=64] {'trk'}, dimensions={2}, use_global_device_ids=true | all-gather | bytes 532480 | tf_op jit(solution)/shard_map/all_gather | solution.py:112
  193.1 8.9 all-to-all-start.3
  202.5 21.9 %all-gather.2.cloned.1.call-done = bf16[4,512,512]{2,1,0:T(8,128)(2,1)} async-done(((bf16[4,128,512]{2,1,0:T(8,128)(2,1)}), bf16[4,512,512]{2,1,0:T(8,128)(2,1)}) %all-gather.2.cloned.1.call-update) | async-done | bytes 2097168 | tf_op jit(solution)/shard_map/all_gather | solution.py:113
  224.3 2.3 convolution_convert_fusion.8
  226.6 13.0 %all-to-all-start = ((bf16[64,8,512]{2,1,0:T(8,128)(2,1)}), bf16[64,8,512]{2,1,0:T(8,128)(2,1)S(1)}, u32[]{:S(2)}, u32[]{:S(2)}) async-start(bf16[64,8,512]{2,1,0:T(8,128)(2,1)} %convolution_convert_fusion.8), calls=%async_computation | async-start | bytes 1048576 | tf_op jit(solution)/shard_map/all_to_all | solution.py:121
  239.7 2.3 convolution_convert_fusion.7
  242.0 16.4 %all-to-all-done = bf16[64,8,512]{2,1,0:T(8,128)(2,1)S(1)} async-done(((bf16[64,8,512]{2,1,0:T(8,128)(2,1)}), bf16[64,8,512]{2,1,0:T(8,128)(2,1)S(1)}, u32[]{:S(2)}, u32[]{:S(2)}) %all-to-all-start) | async-done | bytes 524320 | tf_op jit(solution)/shard_map/all_to_all | solution.py:121
  258.4 6.5 all-to-all-start.1
  265.0 2.3 convolution_convert_fusion.6
  267.3 15.6 %all-to-all-done.1 = bf16[64,8,512]{2,1,0:T(8,128)(2,1)S(1)} async-done(((bf16[64,8,512]{2,1,0:T(8,128)(2,1)}), bf16[64,8,512]{2,1,0:T(8,128)(2,1)S(1)}, u32[]{:S(2)}, u32[]{:S(2)}) %all-to-all-start.1) | async-done | bytes 524320 | tf_op jit(solution)/shard_map/all_to_all | solution.py:122
  282.9 6.7 all-to-all-start.2
  293.1 2.4 reshape.122
  296.9 9.8 all-to-all-done.2
  306.7 2.4 reshape.124
  309.1 2.3 copy.62
  311.4 60.7 %while.16 = (s32[]{:T(128)}, bf16[8,512,64]{1,2,0:T(8,128)(2,1)}, bf16[8,512,64]{1,2,0:T(8,128)(2,1)}, bf16[8,512,64]{1,2,0:T(8,128)(2,1)}, bf16[8,512,64]{1,2,0...) while((s32[]{:T(128)}, bf16[8,512,64]{1,2,0:T(8,128)(2,1)}, ...), condition=%wide.region_6.7_spmd, body=%wide.region_2.6_spmd.sunk | while | flops 206699008 | bytes 11305061 | solution.py:78
  311.9 1.8 fusion.112
  317.2 1.8 fusion.109
  319.5 1.8 fusion.112
  324.8 1.8 fusion.109
  327.1 1.8 fusion.112
  332.4 1.8 fusion.109
  334.7 1.8 fusion.112
  339.9 1.8 fusion.109
  342.3 1.8 fusion.112
  349.9 1.8 fusion.112
  357.5 1.8 fusion.112
  365.0 1.8 fusion.112
  372.1 2.4 copy.65
  375.1 3.8 reduce.1
  379.9 6.5 all-to-all-start.6
  386.4 2.4 copy.64
  388.8 3.8 reduce.2
  393.6 9.5 all-to-all-done.6
  403.1 6.7 all-to-all-start.5
  409.8 2.4 copy.63
  412.2 3.8 reduce.3
  417.1 2.3 fusion.55
  419.9 6.2 all-to-all-done.5
  426.1 6.6 all-to-all-start.4
  434.4 3.6 reshape.149
  439.5 8.9 all-to-all-done.4
  450.2 2.0 fusion.58
  458.0 21.6 %reduce-scatter.2.cloned.1.call-done = bf16[4,128,512]{2,1,0:T(8,128)(2,1)} async-done(((bf16[4,512,512]{2,1,0:T(8,128)(2,1)}), bf16[4,128,512]{2,1,0:T(8,128)(2,1)}) %reduce-scatter.2.cloned.1.call-update) | async-done | bytes 524304 | tf_op jit(solution)/shard_map/reduce_scatter | solution.py:142
  479.6 2.3 copy.69
  481.9 2.8 fusion.64
  484.8 76.2 %psum.7 = f32[512]{0:T(512)S(1)} all-reduce(f32[512]{0:T(512)S(1)} %get-tuple-element.108), channel_id=1, replica_groups=mesh['grp'=4,'trk'=64] {'grp','trk'}, use_global_device_ids=true, to_apply=%region_12.13 | all-reduce | flops 512 | bytes 4096 | tf_op jit(solution)/shard_map/psum | solution.py:146
  562.8 617.9 %all-reduce.3.cloned.1.call-done = f32[4,128,512]{1,0,2:T(4,128)} async-done(((f32[4,128,512]{1,0,2:T(4,128)}), f32[4,128,512]{1,0,2:T(4,128)}) %all-reduce.3.cloned.1.call-update) | async-done | bytes 1048592
  (112 shorter events, 63.0 us)
Async XLA Ops:
  7.2 194.8 %copy-start = (bf16[64,8,512]{2,1,0:T(8,128)(2,1)S(1)}, bf16[64,8,512]{2,1,0:T(8,128)(2,1)}, u32[]{:S(2)}) copy-start(bf16[64,8,512]{2,1,0:T(8,128)(2,1)} %param.6) | copy-start | bytes 1572868
  7.2 217.1 %all-gather.2.cloned.1.call-start = ((), (), s32[]{:S(2)}) async-start(), calls=%async_computation.8 | async-start | bytes 2621440 | tf_op jit(solution)/shard_map/all_gather | solution.py:113
  8.0 216.3 %copy-start.8 = (f32[512]{0:T(512)S(1)}, f32[512]{0:T(512)}, u32[]{:S(2)}) copy-start(f32[512]{0:T(512)} %param.8) | copy-start | bytes 6148
  193.1 33.6 %all-to-all-start.3 = ((bf16[64,8,512]{2,1,0:T(8,128)(2,1)}), bf16[64,8,512]{2,1,0:T(8,128)(2,1)S(1)}, u32[]{:S(2)}, u32[]{:S(2)}) async-start(bf16[64,8,512]{2,1,0:T(8,128)(2,1)} %param.7), calls=%async_computation.3 | async-start | bytes 1048576 | tf_op jit(solution)/shard_map/all_to_all | solution.py:124
  226.6 31.8 %all-to-all-start = ((bf16[64,8,512]{2,1,0:T(8,128)(2,1)}), bf16[64,8,512]{2,1,0:T(8,128)(2,1)S(1)}, u32[]{:S(2)}, u32[]{:S(2)}) async-start(bf16[64,8,512]{2,1,0:T(8,128)(2,1)} %convolution_convert_fusion.8), calls=%async_computation | async-start | bytes 1048576 | tf_op jit(solution)/shard_map/all_to_all | solution.py:121
  258.4 24.4 %all-to-all-start.1 = ((bf16[64,8,512]{2,1,0:T(8,128)(2,1)}), bf16[64,8,512]{2,1,0:T(8,128)(2,1)S(1)}, u32[]{:S(2)}, u32[]{:S(2)}) async-start(bf16[64,8,512]{2,1,0:T(8,128)(2,1)} %convolution_convert_fusion.7), calls=%async_computation.1 | async-start | bytes 1048576 | tf_op jit(solution)/shard_map/all_to_all | solution.py:122
  282.9 9.6 copy-start.2
  282.9 23.8 %all-to-all-start.2 = ((bf16[64,8,512]{2,1,0:T(8,128)(2,1)}), bf16[64,8,512]{2,1,0:T(8,128)(2,1)}, u32[]{:S(2)}, u32[]{:S(2)}) async-start(bf16[64,8,512]{2,1,0:T(8,128)(2,1)} %convolution_convert_fusion.6), calls=%async_computation.2 | async-start | bytes 1048576 | tf_op jit(solution)/shard_map/all_to_all | solution.py:123
  379.9 23.2 %all-to-all-start.6 = ((bf16[64,2,2048]{2,1,0:T(2,128)(2,1)}), bf16[64,2,2048]{2,1,0:T(2,128)(2,1)S(1)}, u32[]{:S(2)}, u32[]{:S(2)}) async-start(bf16[64,2,2048]{2,1,0:T(2,128)(2,1)} %reshape.146), calls=%async_computation.6 | async-start | bytes 1048576 | tf_op jit(solution)/shard_map/all_to_all | solution.py:132
  403.1 22.9 %all-to-all-start.5 = ((bf16[64,2,2048]{2,1,0:T(2,128)(2,1)}), bf16[64,2,2048]{2,1,0:T(2,128)(2,1)}, u32[]{:S(2)}, u32[]{:S(2)}) async-start(bf16[64,2,2048]{2,1,0:T(2,128)(2,1)} %reshape.148), calls=%async_computation.5 | async-start | bytes 1048576 | tf_op jit(solution)/shard_map/all_to_all | solution.py:131
  426.1 22.4 %all-to-all-start.4 = ((bf16[64,2,2048]{2,1,0:T(2,128)(2,1)}), bf16[64,2,2048]{2,1,0:T(2,128)(2,1)S(1)}, u32[]{:S(2)}, u32[]{:S(2)}) async-start(bf16[64,2,2048]{2,1,0:T(2,128)(2,1)} %reshape.150), calls=%async_computation.4 | async-start | bytes 1048576 | tf_op jit(solution)/shard_map/all_to_all | solution.py:130
  432.6 47.0 %reduce-scatter.2.cloned.1.call-start = ((), (), s32[]{:S(2)}) async-start(), calls=%async_computation.9 | async-start | bytes 2621440 | tf_op jit(solution)/shard_map/reduce_scatter | solution.py:142
  450.2 2.0 copy-start.4
  450.2 2.0 copy-start.6
  450.2 2.0 copy-start.7
  453.9 0.7 copy-start.9
  453.9 726.9 %all-reduce.3.cloned.1.call-start = ((), (), s32[]{:S(2)}) async-start(), calls=%async_computation.10 | async-start | bytes 2097152
  455.8 1.3 copy-start.1
  457.1 24.8 %copy-start.5 = (bf16[1,512,512]{2,1,0:T(8,128)(2,1)S(1)}, bf16[1,512,512]{2,1,0:T(8,128)(2,1)}, u32[]{:S(2)}) copy-start(bf16[1,512,512]{2,1,0:T(8,128)(2,1)} %copy.94) | copy-start | bytes 1572868
  481.9 79.7 %copy-start.3 = (bf16[64,8,512]{2,1,0:T(8,128)(2,1)S(1)}, bf16[64,8,512]{2,1,0:T(8,128)(2,1)}, u32[]{:S(2)}) copy-start(bf16[64,8,512]{2,1,0:T(8,128)(2,1)} %param.7) | copy-start | bytes 1572868
Sparse Core Ops, SparseCore 0:
  193.2 31.0 all-gather.1
  454.0 25.5 reduce-scatter.1
  482.4 698.3 all-reduce.2
where the time goes:
time: 1190 us
  waiting for transfers between devices  728 us (61%)
  blocking collectives  260 us (22%)
  matrix products  75.3 us (6%)
  starting transfers between devices  55.3 us (5%)
  local copies, waits for them, and re-layouts  35.4 us (3%)
  other arithmetic  19.9 us (2%)
  between operations  14.7 us (1%)
    unnamed x4, waiting for transfers between devices  618 us
    all_gather x1, blocking collectives, shards(): w_part = lax.all_gather(weights, 'trk', axis=2, tiled=True)  184 us
    psum x1, blocking collectives, shards(): gain_sum = lax.psum(gain_term, ('grp', 'trk'))  76.2 us
  transfers between devices with their start and end apart: 10, of which 9 were waited for; matrix products, arithmetic and copies ran while one was open for 4% of the time, Pallas kernels for 0%

commit v1 on v0

--- a/solution.py
+++ b/solution.py
@@ -109,7 +109,9 @@
 
 
 def shards(fields, upstream, ln_gain, weights):
-    w_part = lax.all_gather(weights, "trk", axis=2, tiled=True)
+    w_part = jnp.concatenate(
+        lax.all_to_all(jnp.stack([weights] * lax.axis_size("trk")), "trk", 0, 0), axis=2
+    )
     w_full = lax.all_gather(w_part, "grp", axis=1, tiled=True)
     w_in = w_full[:3]
     w_out = w_full[3]

time: 1190 us -> 1040 us (0.87)
  blocking collectives: 260 us -> 109 us
    all_gather x1 -> x0, blocking collectives: 184 us -> none  [shards(): w_part = lax.all_gather(weights, 'trk', axis=2, tiled=True)]
    all_to_all x0 -> x1, blocking collectives: none -> 33 us  [shards(): lax.all_to_all(jnp.stack([weights] * lax.axis_size('trk')), 'trk', 0, 0)]
where the time goes in v1:
time: 1040 us
  waiting for transfers between devices  730 us (70%)
  blocking collectives  109 us (10%)
  matrix products  75.1 us (7%)
  starting transfers between devices  52.2 us (5%)
  local copies, waits for them, and re-layouts  34.6 us (3%)
  other arithmetic  21 us (2%)
  between operations  14.7 us (1%)
    unnamed x4, waiting for transfers between devices  617 us
    psum x1, blocking collectives, shards(): gain_sum = lax.psum(gain_term, ('grp', 'trk'))  76.3 us
    all_to_all x1, blocking collectives, shards(): lax.all_to_all(jnp.stack([weights] * lax.axis_size('trk')), 'trk', 0, 0)  33 us
    all_gather x1, waiting for transfers between devices, shards(): w_full = lax.all_gather(w_part, 'grp', axis=1, tiled=True)  23.9 us
    reduce_scatter x1, waiting for transfers between devices, shards(): lax.psum_scatter(raw_grad.astype(jnp.bfloat16), 'grp', scatter_dimension=...  22.4 us
  transfers between devices with their start and end apart: 10, of which 9 were waited for; matrix products, arithmetic and copies ran while one was open for 4% of the time, Pallas kernels for 0%

profile of v1, /device:TPU:2, one launch (start us, length us, event | category | flops | bytes accessed | tf_op | source)
XLA Modules:
  0.0 1036.5 jit_solution(13983332610390034648)
XLA Ops:
  8.0 33.0 %all_to_all.77 = bf16[64,4,128,8]{2,3,1,0:T(8,128)(2,1)S(1)} all-to-all(bf16[64,4,128,8]{2,3,1,0:T(8,128)(2,1)S(1)} %stack.25), channel_id=1, replica_groups=mesh['grp'=4,'trk'=64] {'trk'}, dimensions={0} | all-to-all | bytes 1048576 | tf_op jit(solution)/shard_map/all_to_all | solution.py:113
  42.1 6.5 all-to-all-start.4
  49.1 23.9 %all-gather.2.cloned.1.call-done = bf16[4,512,512]{2,1,0:T(8,128)(2,1)} async-done(((bf16[4,128,512]{2,1,0:T(8,128)(2,1)}), bf16[4,512,512]{2,1,0:T(8,128)(2,1)}) %all-gather.2.cloned.1.call-update) | async-done | bytes 2097168 | tf_op jit(solution)/shard_map/all_gather | solution.py:115
  73.0 2.3 convolution_convert_fusion.8
  75.4 12.3 %all-to-all-start.1 = ((bf16[64,8,512]{2,1,0:T(8,128)(2,1)}), bf16[64,8,512]{2,1,0:T(8,128)(2,1)S(1)}, u32[]{:S(2)}, u32[]{:S(2)}) async-start(bf16[64,8,512]{2,1,0:T(8,128)(2,1)} %convolution_convert_fusion.8), calls=%async_computation.1 | async-start | bytes 1048576 | tf_op jit(solution)/shard_map/all_to_all | solution.py:123
  87.6 2.3 convolution_convert_fusion.7
  90.0 16.4 %all-to-all-done.1 = bf16[64,8,512]{2,1,0:T(8,128)(2,1)S(1)} async-done(((bf16[64,8,512]{2,1,0:T(8,128)(2,1)}), bf16[64,8,512]{2,1,0:T(8,128)(2,1)S(1)}, u32[]{:S(2)}, u32[]{:S(2)}) %all-to-all-start.1) | async-done | bytes 524320 | tf_op jit(solution)/shard_map/all_to_all | solution.py:123
  106.4 6.5 all-to-all-start.2
  112.9 2.3 convolution_convert_fusion.6
  115.3 15.6 %all-to-all-done.2 = bf16[64,8,512]{2,1,0:T(8,128)(2,1)S(1)} async-done(((bf16[64,8,512]{2,1,0:T(8,128)(2,1)}), bf16[64,8,512]{2,1,0:T(8,128)(2,1)S(1)}, u32[]{:S(2)}, u32[]{:S(2)}) %all-to-all-start.2) | async-done | bytes 524320 | tf_op jit(solution)/shard_map/all_to_all | solution.py:124
  130.8 6.7 all-to-all-start.3
  141.1 2.4 reshape.132
  144.8 9.8 all-to-all-done.3
  154.6 2.4 reshape.134
  157.0 2.3 copy.62
  159.4 60.7 %while.16 = (s32[]{:T(128)}, bf16[8,512,64]{1,2,0:T(8,128)(2,1)}, bf16[8,512,64]{1,2,0:T(8,128)(2,1)}, bf16[8,512,64]{1,2,0:T(8,128)(2,1)}, bf16[8,512,64]{1,2,0...) while((s32[]{:T(128)}, bf16[8,512,64]{1,2,0:T(8,128)(2,1)}, ...), condition=%wide.region_6.7_spmd, body=%wide.region_2.6_spmd.sunk | while | flops 206699008 | bytes 11305061 | solution.py:78
  159.9 1.8 fusion.112
  167.5 1.8 fusion.112
  175.1 1.8 fusion.112
  182.7 1.8 fusion.112
  187.9 1.8 fusion.109
  190.2 1.8 fusion.112
  195.5 1.8 fusion.109
  197.8 1.8 fusion.112
  203.1 1.8 fusion.109
  205.4 1.8 fusion.112
  213.0 1.8 fusion.112
  220.1 2.4 copy.65
  223.0 3.8 reduce.1
  227.8 6.5 all-to-all-start.7
  234.4 2.4 copy.64
  236.8 3.8 reduce.2
  241.6 9.4 all-to-all-done.7
  251.1 6.7 all-to-all-start.6
  257.8 2.4 copy.63
  260.2 3.8 reduce.3
  265.0 2.3 fusion.55
  267.8 6.1 all-to-all-done.6
  274.0 6.6 all-to-all-start.5
  282.4 3.6 reshape.159
  287.5 8.8 all-to-all-done.5
  298.1 2.0 fusion.58
  305.1 22.4 %reduce-scatter.2.cloned.1.call-done = bf16[4,128,512]{2,1,0:T(8,128)(2,1)} async-done(((bf16[4,512,512]{2,1,0:T(8,128)(2,1)}), bf16[4,128,512]{2,1,0:T(8,128)(2,1)}) %reduce-scatter.2.cloned.1.call-update) | async-done | bytes 524304 | tf_op jit(solution)/shard_map/reduce_scatter | solution.py:144
  327.5 2.3 copy.69
  329.7 2.6 fusion.64
  332.4 76.3 %psum.7 = f32[512]{0:T(512)S(1)} all-reduce(f32[512]{0:T(512)S(1)} %get-tuple-element.108), channel_id=1, replica_groups=mesh['grp'=4,'trk'=64] {'grp','trk'}, use_global_device_ids=true, to_apply=%region_12.13 | all-reduce | flops 512 | bytes 4096 | tf_op jit(solution)/shard_map/psum | solution.py:148
  409.3 2.3 add_convert_fusion
  411.5 617.1 %all-reduce.3.cloned.1.call-done = f32[4,128,512]{1,0,2:T(4,128)} async-done(((f32[4,128,512]{1,0,2:T(4,128)}), f32[4,128,512]{1,0,2:T(4,128)}) %all-reduce.3.cloned.1.call-update) | async-done | bytes 1048592
  (111 shorter events, 62.9 us)
Async XLA Ops:
  7.2 65.9 %all-gather.2.cloned.1.call-start = ((), (), s32[]{:S(2)}) async-start(), calls=%async_computation.9 | async-start | bytes 2621440 | tf_op jit(solution)/shard_map/all_gather | solution.py:115
  41.0 7.6 copy-start
  41.1 32.0 %copy-start.7 = (f32[512]{0:T(512)S(1)}, f32[512]{0:T(512)}, u32[]{:S(2)}) copy-start(f32[512]{0:T(512)} %param.8) | copy-start | bytes 6148
  42.1 33.2 %all-to-all-start.4 = ((bf16[64,8,512]{2,1,0:T(8,128)(2,1)}), bf16[64,8,512]{2,1,0:T(8,128)(2,1)S(1)}, u32[]{:S(2)}, u32[]{:S(2)}) async-start(bf16[64,8,512]{2,1,0:T(8,128)(2,1)} %param.7), calls=%async_computation.4 | async-start | bytes 1048576 | tf_op jit(solution)/shard_map/all_to_all | solution.py:126
  75.4 31.0 %all-to-all-start.1 = ((bf16[64,8,512]{2,1,0:T(8,128)(2,1)}), bf16[64,8,512]{2,1,0:T(8,128)(2,1)S(1)}, u32[]{:S(2)}, u32[]{:S(2)}) async-start(bf16[64,8,512]{2,1,0:T(8,128)(2,1)} %convolution_convert_fusion.8), calls=%async_computation.1 | async-start | bytes 1048576 | tf_op jit(solution)/shard_map/all_to_all | solution.py:123
  106.4 24.4 %all-to-all-start.2 = ((bf16[64,8,512]{2,1,0:T(8,128)(2,1)}), bf16[64,8,512]{2,1,0:T(8,128)(2,1)S(1)}, u32[]{:S(2)}, u32[]{:S(2)}) async-start(bf16[64,8,512]{2,1,0:T(8,128)(2,1)} %convolution_convert_fusion.7), calls=%async_computation.2 | async-start | bytes 1048576 | tf_op jit(solution)/shard_map/all_to_all | solution.py:124
  130.8 9.6 copy-start.2
  130.8 23.8 %all-to-all-start.3 = ((bf16[64,8,512]{2,1,0:T(8,128)(2,1)}), bf16[64,8,512]{2,1,0:T(8,128)(2,1)}, u32[]{:S(2)}, u32[]{:S(2)}) async-start(bf16[64,8,512]{2,1,0:T(8,128)(2,1)} %convolution_convert_fusion.6), calls=%async_computation.3 | async-start | bytes 1048576 | tf_op jit(solution)/shard_map/all_to_all | solution.py:125
  227.8 23.2 %all-to-all-start.7 = ((bf16[64,2,2048]{2,1,0:T(2,128)(2,1)}), bf16[64,2,2048]{2,1,0:T(2,128)(2,1)S(1)}, u32[]{:S(2)}, u32[]{:S(2)}) async-start(bf16[64,2,2048]{2,1,0:T(2,128)(2,1)} %reshape.156), calls=%async_computation.7 | async-start | bytes 1048576 | tf_op jit(solution)/shard_map/all_to_all | solution.py:134
  251.1 22.9 %all-to-all-start.6 = ((bf16[64,2,2048]{2,1,0:T(2,128)(2,1)}), bf16[64,2,2048]{2,1,0:T(2,128)(2,1)}, u32[]{:S(2)}, u32[]{:S(2)}) async-start(bf16[64,2,2048]{2,1,0:T(2,128)(2,1)} %reshape.158), calls=%async_computation.6 | async-start | bytes 1048576 | tf_op jit(solution)/shard_map/all_to_all | solution.py:133
  274.0 22.3 %all-to-all-start.5 = ((bf16[64,2,2048]{2,1,0:T(2,128)(2,1)}), bf16[64,2,2048]{2,1,0:T(2,128)(2,1)S(1)}, u32[]{:S(2)}, u32[]{:S(2)}) async-start(bf16[64,2,2048]{2,1,0:T(2,128)(2,1)} %reshape.160), calls=%async_computation.5 | async-start | bytes 1048576 | tf_op jit(solution)/shard_map/all_to_all | solution.py:132
  280.6 46.9 %reduce-scatter.2.cloned.1.call-start = ((), (), s32[]{:S(2)}) async-start(), calls=%async_computation.10 | async-start | bytes 2621440 | tf_op jit(solution)/shard_map/reduce_scatter | solution.py:144
  298.1 2.0 copy-start.3
  298.1 2.0 copy-start.5
  298.1 2.0 copy-start.6
  301.7 0.7 copy-start.8
  301.8 726.8 %all-reduce.3.cloned.1.call-start = ((), (), s32[]{:S(2)}) async-start(), calls=%async_computation.11 | async-start | bytes 2097152
  303.6 1.3 copy-start.1
  305.0 24.8 %copy-start.4 = (bf16[1,512,512]{2,1,0:T(8,128)(2,1)S(1)}, bf16[1,512,512]{2,1,0:T(8,128)(2,1)}, u32[]{:S(2)}) copy-start(bf16[1,512,512]{2,1,0:T(8,128)(2,1)} %copy.96) | copy-start | bytes 1572868
Sparse Core Ops, SparseCore 0:
  42.2 30.7 all-gather.1
  301.9 25.5 reduce-scatter.1
  330.3 698.2 all-reduce.2
